TPU v7x, 32 devices: a whole 2x2x4 slice. The times are simulated.
32 devices in a mesh: tm: 2 (over y), pairs: 16 (over z, x, core).
Axes of the slice: x: 2, y: 2, z: 4, core: 2. Of those that a mesh axis runs over, the one named last changes fastest.
Arguments:
- records: bfloat16 [2, 512, 128, 2048], P('tm', 'pairs')
- source_map: int32 [2, 512], P('tm'), may hold values from 0 to 511, each once within a row
- pair_blocks: int32 [16, 6, 2], P('pairs'), may hold values from -1 to 31, as said below
Outputs:
- stacks: float32 [96, 16, 2, 128, 128], P('pairs', 'tm')
Inputs may be any that keep to these rules, and one draw needn't show every extreme that they name: `pair_blocks`: each pair slot holds blocks i <= j with j - i <= 2, or -1 and -1 when empty; every such pair appears in exactly one slot; some owner has all 6 slots filled. `source_map`: each row is a permutation: every slot of a time group holds exactly one window of one channel block.
All inputs are finite; a program needn't handle non-finite values.
Results may differ from a plain program's by a relative error of at most 0.0056.
Values may be sent and summed in bfloat16 or wider, within the bound.
A program may use at most 128 MiB of HBM per device.

v0:
```python
import math
import jax
import jax.numpy as jnp
from jax import lax
from jax.sharding import PartitionSpec as P

NB = 32
BINS = 16
FIRST_BIN = 64
WIN = 16


def transform_table(length):
    samples = jnp.arange(length, dtype=jnp.int32)
    bin_index = FIRST_BIN + jnp.arange(BINS, dtype=jnp.int32)
    phases = samples[:, None] * bin_index[None, :] % length
    angles = 2.0 * math.pi / length * phases.astype(jnp.float32)
    taper = 0.5 - 0.5 * jnp.cos(2.0 * math.pi / length * samples.astype(jnp.float32))
    weight_col = (taper / math.sqrt(length))[:, None]
    return jnp.concatenate(
        [jnp.cos(angles) * weight_col, -jnp.sin(angles) * weight_col], axis=1
    ).astype(jnp.bfloat16)


def whiten_spectra(windows, table):
    transformed = jnp.einsum("scn,nk->skc", windows, table, preferred_element_type=jnp.float32)
    real_part = transformed[:, :BINS]
    imag_part = transformed[:, BINS:]
    power = jnp.mean(real_part * real_part + imag_part * imag_part, axis=2, keepdims=True)
    inverse = 1.0 / jnp.sqrt(power + 1e-06)
    return (transformed * jnp.concatenate([inverse, inverse], axis=1)).astype(jnp.bfloat16)


def cross_stack(left_spec, right_spec):
    real_sum = jnp.einsum(
        "pwfi,pwfj->pfij",
        left_spec[:, :, 0],
        right_spec[:, :, 0],
        preferred_element_type=jnp.float32,
    )
    real_sum = real_sum + jnp.einsum(
        "pwfi,pwfj->pfij",
        left_spec[:, :, 1],
        right_spec[:, :, 1],
        preferred_element_type=jnp.float32,
    )
    imag_sum = jnp.einsum(
        "pwfi,pwfj->pfij",
        left_spec[:, :, 1],
        right_spec[:, :, 0],
        preferred_element_type=jnp.float32,
    )
    imag_sum = imag_sum - jnp.einsum(
        "pwfi,pwfj->pfij",
        left_spec[:, :, 0],
        right_spec[:, :, 1],
        preferred_element_type=jnp.float32,
    )
    return jnp.stack([real_sum, imag_sum], axis=2)


def per_device(records, source_map, pair_blocks):
    table = transform_table(records.shape[3])
    local_spec = whiten_spectra(records[0], table)
    channels = local_spec.shape[2]
    blocks = pair_blocks[0]
    slot_count = blocks.shape[0]
    valid = (blocks[:, 0] >= 0).astype(jnp.float32)
    safe_blocks = jnp.maximum(blocks, 0)
    window_ids = jnp.arange(WIN, dtype=jnp.int32)
    columns = window_ids[None, None, :] * NB + safe_blocks[:, :, None]
    wanted = jnp.take(source_map[0], columns.reshape(-1))
    piece = lax.all_gather(local_spec, "pairs", axis=0, tiled=True)
    row_ids = jnp.arange(piece.shape[0], dtype=jnp.int32)
    onehot = (wanted[:, None] == row_ids[None, :]).astype(jnp.bfloat16)
    collected = jnp.einsum("nr,rkc->nkc", onehot, piece, preferred_element_type=jnp.float32)
    picked = collected.astype(jnp.bfloat16)
    chosen = picked.reshape(slot_count, 2, WIN, 2, BINS, channels)
    norm_factor = 1.0 / math.sqrt(WIN * lax.axis_size("tm"))
    partial_stack = cross_stack(chosen[:, 0], chosen[:, 1])
    summed = lax.psum_scatter(partial_stack, "tm", scatter_dimension=1, tiled=True)
    return summed * (valid * norm_factor)[:, None, None, None, None]


def solution(mesh):
    return jax.shard_map(
        per_device,
        mesh=mesh,
        in_specs=(P("tm", "pairs", None, None), P("tm", None), P("pairs", None, None)),
        out_specs=P("pairs", "tm", None, None, None),
        check_vma=False,
    )
```

profile of v0, /device:TPU:0, one launch (start us, length us, event | category | flops | bytes accessed | tf_op | source)
XLA Modules:
  0.0 275.5 jit_solution(10862450789281669629)
XLA Ops:
  6.5 0.0 all-gather.2.cloned.1.call-start
  6.5 0.1 subtract_multiply_fusion
  6.6 0.6 multiply_convert_fusion.2
  7.2 0.0 copy-start.2
  7.2 8.6 %fusion.7 = f32[32,32,128]{2,1,0:T(8,128)S(1)} fusion(bf16[1,32,128,2048]{3,2,1,0:T(8,128)(2,1)} %param.3, bf16[2048,16]{0,1:T(8,128)(2,1)S(1)} %get-tuple-element.8, bf16[2048,16]{0,1:T(8,128)(2,1)S(1)} %get-tuple-element.7), kind=kOutput, calls=%fused_computation.11 | convolution fusion | flops 537133056 | bytes 17432576 | tf_op jit(solution)/shard_map/scn,nk->skc/dot_general | solution.py:26
  15.8 0.2 fusion.15
  16.0 0.1 maximum_bitcast_fusion.2
  16.1 0.9 multiply_convert_fusion
  17.0 0.0 all-gather.2.cloned.1.call-update
  17.0 0.0 reduce-scatter.5.cloned.1.call-start
  17.1 0.1 copy.14
  17.2 0.1 broadcast_add_fusion
  17.2 0.1 add.102
  17.3 0.1 add.99
  17.4 1.8 gather_fusion
  19.2 51.1 %all-gather.2.cloned.1.call-done = bf16[512,32,128]{2,1,0:T(8,128)(2,1)} async-done(((bf16[32,32,128]{2,1,0:T(8,128)(2,1)}), bf16[512,32,128]{2,1,0:T(8,128)(2,1)}) %all-gather.2.cloned.1.call-update) | async-done | bytes 4194320 | tf_op jit(solution)/shard_map/all_gather | solution.py:73
  70.4 4.0 %fusion.4 = bf16[192,32,128]{2,0,1:T(8,128)(2,1)S(1)} fusion(bf16[512,32,128]{2,1,0:T(8,128)(2,1)} %all-gather.2.cloned.1.call-done, s32[192]{0:T(256)S(1)} %and_select_fusion), kind=kOutput, calls=%fused_computation.10 | convolution fusion | flops 806191104 | bytes 5767936 | tf_op jit(solution)/shard_map/nr,rkc->nkc/dot_general | solution.py:76
  74.4 0.3 fusion.27
  74.7 0.4 copy_bitcast_fusion.1
  75.1 1.0 fusion.12
  76.1 1.0 fusion.13
  77.1 1.0 add_bitcast_fusion
  78.2 3.7 %subtract_bitcast_fusion = f32[6,16,1,128,128]{4,3,1,0,2:T(8,128)} fusion(f32[6,16,128,128]{3,2,1,0:T(8,128)S(1)} %fusion.13, bf16[6,16,2,16,128]{4,1,3,0,2:T(8,128)(2,1)S(1)} %get-tuple-element.10, bf16[6,16,2,16,128]{4,1,3,0,2:T(8,128)(2,1)S(1)} %get-tuple-element.9), kind=kOutput, calls=%fused_computation.6 | convolution fusion | flops 51904512 | bytes 13369344 | tf_op jit(solution)/shard_map/pwfi,pwfj->pfij/dot_general | solution.py:53
  81.9 9.6 %pad_maximum_fusion = f32[6,16,2,128,128]{4,3,1,0,2:T(8,128)} fusion(f32[6,16,1,128,128]{4,3,1,0,2:T(8,128)} %subtract_bitcast_fusion, f32[6,16,1,128,128]{4,3,1,0,2:T(8,128)S(1)} %add_bitcast_fusion), kind=kLoop, calls=%fused_computation.4 | loop fusion | flops 3145728 | bytes 25165824 | tf_op jit(solution)/shard_map/stack | solution.py:59
  91.5 11.3 %copy.19 = f32[6,16,2,128,128]{4,3,0,2,1:T(8,128)} copy(f32[6,16,2,128,128]{4,3,1,0,2:T(8,128)} %pad_maximum_fusion) | data formatting | bytes 25165824
  102.8 14.4 %copy.33 = f32[2,8,1536,128]{3,1,2,0:T(8,128)} copy(f32[2,8,1536,128]{3,2,1,0:T(8,128)} %bitcast.64) | data formatting | bytes 25165824
  117.2 0.0 reduce-scatter.5.cloned.1.call-update
  117.2 143.1 %reduce-scatter.5.cloned.1.call-done = f32[8,196608]{1,0:T(8,128)} async-done(((f32[16,196608]{1,0:T(8,128)}), f32[8,196608]{1,0:T(8,128)}) %reduce-scatter.5.cloned.1.call-update) | async-done | bytes 6291472
  260.4 4.0 %copy.24 = f32[1,8,1536,128]{3,2,1,0:T(8,128)S(1)} copy(f32[1,8,1536,128]{3,1,2,0:T(8,128)} %bitcast.66) | data formatting | bytes 12582912
  264.4 0.0 copy-start.1
  264.4 1.1 copy_multiply_fusion
  265.5 3.1 %copy.18 = f32[6,8,2,128,128]{4,3,2,1,0:T(8,128)} copy(f32[6,8,2,128,128]{4,3,1,0,2:T(8,128)S(1)} %copy_multiply_fusion) | data formatting | bytes 12582912 | tf_op jit(solution)/shard_map/mul | solution.py:82
  (12 shorter events, 0.0 us)
Async XLA Ops:
  6.5 10.9 %copy-start = (s32[1,512]{1,0:T(1,128)S(1)}, s32[1,512]{1,0:T(1,128)}, u32[]{:S(2)}) copy-start(s32[1,512]{1,0:T(1,128)} %param.4) | copy-start | bytes 6148
  6.5 63.9 %all-gather.2.cloned.1.call-start = ((), (), s32[]{:S(2)}) async-start(), calls=%async_computation.1 | async-start | bytes 4456448 | tf_op jit(solution)/shard_map/all_gather | solution.py:73
  7.2 9.8 %copy-start.2 = (s32[1,6,2]{1,2,0:T(2,128)S(1)}, s32[1,6,2]{1,2,0:T(2,128)}, u32[]{:S(2)}) copy-start(s32[1,6,2]{1,2,0:T(2,128)} %param.5) | copy-start | bytes 148
  17.0 243.4 %reduce-scatter.5.cloned.1.call-start = ((), (), s32[]{:S(2)}) async-start(), calls=%async_computation.2 | async-start | bytes 18874368
  264.4 4.3 %copy-start.1 = (s32[1,512]{1,0:T(1,128)S(1)}, s32[1,512]{1,0:T(1,128)}, u32[]{:S(2)}) copy-start(s32[1,512]{1,0:T(1,128)} %param.4) | copy-start | bytes 6148
Sparse Core Ops, SparseCore 0:
  17.1 53.2 all-gather.1
  117.3 142.9 reduce-scatter.4
where the time goes:
time: 276 us
  waiting for transfers between devices  194 us (70%)
  local copies, waits for them, and re-layouts  35.6 us (13%)
  matrix products  19.3 us (7%)
  between operations  13.6 us (5%)
  other arithmetic  12.7 us (5%)
    unnamed x3, waiting for transfers between devices  143 us
    all_gather x1, waiting for transfers between devices, per_device(): piece = lax.all_gather(local_spec, 'pairs', axis=0, tiled=True)  51.1 us
    unnamed x9, local copies, waits for them, and re-layouts  29.7 us
    another operation x1, other arithmetic, cross_stack(): return jnp.stack([real_sum, imag_sum], axis=2)  9.6 us
    dot_general x1, matrix products, whiten_spectra(): jnp.einsum('scn,nk->skc', windows, table, preferred_element_type=jnp.floa...  8.57 us
  transfers between devices with their start and end apart: 2, of which 2 were waited for; matrix products, arithmetic and copies ran while one was open for 1% of the time, Pallas kernels for 0%

commit v1 on v0

--- a/solution.py
+++ b/solution.py
@@ -8,6 +8,19 @@
 BINS = 16
 FIRST_BIN = 64
 WIN = 16
+
+
+def gather_around(shard, axis, dim):
+    ways = lax.axis_size(axis)
+    up = [(d, (d + 1) % ways) for d in range(ways)]
+    down = [(d, (d - 1) % ways) for d in range(ways)]
+    earlier, later = ([shard], [shard])
+    for _ in range(ways // 2):
+        earlier.append(lax.ppermute(earlier[-1], axis, up))
+    for _ in range((ways - 1) // 2):
+        later.append(lax.ppermute(later[-1], axis, down))
+    line = jnp.concatenate([*earlier[::-1], *later[1:]], axis=dim)
+    return jnp.roll(line, (lax.axis_index(axis) - ways // 2) * shard.shape[dim], axis=dim)
 
 
 def transform_table(length):
@@ -70,7 +83,7 @@
     window_ids = jnp.arange(WIN, dtype=jnp.int32)
     columns = window_ids[None, None, :] * NB + safe_blocks[:, :, None]
     wanted = jnp.take(source_map[0], columns.reshape(-1))
-    piece = lax.all_gather(local_spec, "pairs", axis=0, tiled=True)
+    piece = gather_around(local_spec, "pairs", 0)
     row_ids = jnp.arange(piece.shape[0], dtype=jnp.int32)
     onehot = (wanted[:, None] == row_ids[None, :]).astype(jnp.bfloat16)
     collected = jnp.einsum("nr,rkc->nkc", onehot, piece, preferred_element_type=jnp.float32)

time: 276 us -> 299 us (1.083)
  starting transfers between devices: 0.04 us -> 32.2 us
  waiting for transfers between devices: 194 us -> 180 us
  local copies, waits for them, and re-layouts: 35.6 us -> 42.9 us
    all_gather x1 -> x0, waiting for transfers between devices: 51.1 us -> none  [per_device(): piece = lax.all_gather(local_spec, 'pairs', axis=0, tiled=True)]
    ppermute x0 -> x15, waiting for transfers between devices: none -> 36 us  [the longest x8 36 us: gather_around(): earlier.append(lax.ppermute(earlier[-1], axis, up))]
    ppermute x0 -> x15, starting transfers between devices: none -> 32.2 us  [the longest x7 31.6 us: gather_around(): later.append(lax.ppermute(later[-1], axis, down))]
    unnamed x9 -> x38, local copies, waits for them, and re-layouts: 29.7 us -> 36.4 us
    unnamed x3 -> x2, waiting for transfers between devices: 143 us -> 144 us
  transfers between devices with their start and end apart: 2 -> 16, of which waited for: 2 -> 9; matrix products, arithmetic and copies ran while one was open for 1% -> 2% of each run, Pallas kernels for 0% -> 0%
where the time goes in v1:
time: 299 us
  waiting for transfers between devices  180 us (60%)
  local copies, waits for them, and re-layouts  42.9 us (14%)
  starting transfers between devices  32.2 us (11%)
  matrix products  17.2 us (6%)
  between operations  13.8 us (5%)
  other arithmetic  12.5 us (4%)
    unnamed x2, waiting for transfers between devices  144 us
    unnamed x38, local copies, waits for them, and re-layouts  36.4 us
    ppermute x8, waiting for transfers between devices, gather_around(): earlier.append(lax.ppermute(earlier[-1], axis, up))  36 us
    ppermute x7, starting transfers between devices, gather_around(): later.append(lax.ppermute(later[-1], axis, down))  31.6 us
    another operation x1, other arithmetic, cross_stack(): return jnp.stack([real_sum, imag_sum], axis=2)  9.62 us
    dot_general x1, matrix products, whiten_spectra(): jnp.einsum('scn,nk->skc', windows, table, preferred_element_type=jnp.floa...  8.57 us
  transfers between devices with their start and end apart: 16, of which 9 were waited for; matrix products, arithmetic and copies ran while one was open for 2% of the time, Pallas kernels for 0%

profile of v1, /device:TPU:0, one launch (start us, length us, event | category | flops | bytes accessed | tf_op | source)
XLA Modules:
  0.0 299.0 jit_solution(6664186120410779246)
XLA Ops:
  7.2 8.6 %fusion.7 = f32[32,32,128]{2,1,0:T(8,128)S(1)} fusion(bf16[1,32,128,2048]{3,2,1,0:T(8,128)(2,1)} %param.3, bf16[2048,16]{0,1:T(8,128)(2,1)S(1)} %get-tuple-element.8, bf16[2048,16]{0,1:T(8,128)(2,1)S(1)} %get-tuple-element.7), kind=kOutput, calls=%fused_computation.11 | convolution fusion | flops 537133056 | bytes 17432576 | tf_op jit(solution)/shard_map/scn,nk->skc/dot_general | solution.py:39
  16.8 9.0 %collective-permute-done = bf16[32,32,128]{2,1,0:T(8,128)(2,1)S(1)} collective-permute-done((bf16[32,32,128]{2,1,0:T(8,128)(2,1)S(1)}, bf16[32,32,128]{2,1,0:T(8,128)(2,1)S(1)}, u32[]{:S(2)}, u32[]{:S(2)}) %collective-permute-start) | collective-permute-done | bytes 262176 | tf_op jit(solution)/shard_map/ppermute | solution.py:19
  25.8 4.4 %collective-permute-start.8 = (bf16[32,32,128]{2,1,0:T(8,128)(2,1)S(1)}, bf16[32,32,128]{2,1,0:T(8,128)(2,1)S(1)}, u32[]{:S(2)}, u32[]{:S(2)}) collective-permute-start(bf16[32,32,128]{2,1,0:T(8,128)(2,1)S(1)} %multiply_convert_fusion), channel_id=1, source_target_pairs={{0,15},{1,0},{2,1},{3,2},{4,3},{5,4},{6,5},{7,6},{8,7},{9,8},{10,9... | collective-permute-start | bytes 786440 | tf_op jit(solution)/shard_map/ppermute | solution.py:21
  30.2 4.1 %collective-permute-done.1 = bf16[32,32,128]{2,1,0:T(8,128)(2,1)S(1)} collective-permute-done((bf16[32,32,128]{2,1,0:T(8,128)(2,1)S(1)}, bf16[32,32,128]{2,1,0:T(8,128)(2,1)S(1)}, u32[]{:S(2)}, u32[]{:S(2)}) %collective-permute-start.1) | collective-permute-done | bytes 262176 | tf_op jit(solution)/shard_map/ppermute | solution.py:19
  34.3 4.5 %collective-permute-start.9 = (bf16[32,32,128]{2,1,0:T(8,128)(2,1)S(1)}, bf16[32,32,128]{2,1,0:T(8,128)(2,1)S(1)}, u32[]{:S(2)}, u32[]{:S(2)}) collective-permute-start(bf16[32,32,128]{2,1,0:T(8,128)(2,1)S(1)} %collective-permute-done.8), channel_id=1, source_target_pairs={{0,15},{1,0},{2,1},{3,2},{4,3},{5,4},{6,5},{7,6},{8,7},{9,8},{10,9... | collective-permute-start | bytes 786440 | tf_op jit(solution)/shard_map/ppermute | solution.py:21
  38.8 4.1 %collective-permute-done.2 = bf16[32,32,128]{2,1,0:T(8,128)(2,1)S(1)} collective-permute-done((bf16[32,32,128]{2,1,0:T(8,128)(2,1)S(1)}, bf16[32,32,128]{2,1,0:T(8,128)(2,1)S(1)}, u32[]{:S(2)}, u32[]{:S(2)}) %collective-permute-start.2) | collective-permute-done | bytes 262176 | tf_op jit(solution)/shard_map/ppermute | solution.py:19
  42.9 4.5 %collective-permute-start.10 = (bf16[32,32,128]{2,1,0:T(8,128)(2,1)S(1)}, bf16[32,32,128]{2,1,0:T(8,128)(2,1)S(1)}, u32[]{:S(2)}, u32[]{:S(2)}) collective-permute-start(bf16[32,32,128]{2,1,0:T(8,128)(2,1)S(1)} %collective-permute-done.9), channel_id=1, source_target_pairs={{0,15},{1,0},{2,1},{3,2},{4,3},{5,4},{6,5},{7,6},{8,7},{9,8},{10,9... | collective-permute-start | bytes 786440 | tf_op jit(solution)/shard_map/ppermute | solution.py:21
  47.4 4.1 %collective-permute-done.3 = bf16[32,32,128]{2,1,0:T(8,128)(2,1)S(1)} collective-permute-done((bf16[32,32,128]{2,1,0:T(8,128)(2,1)S(1)}, bf16[32,32,128]{2,1,0:T(8,128)(2,1)S(1)}, u32[]{:S(2)}, u32[]{:S(2)}) %collective-permute-start.3) | collective-permute-done | bytes 262176 | tf_op jit(solution)/shard_map/ppermute | solution.py:19
  51.5 4.5 %collective-permute-start.11 = (bf16[32,32,128]{2,1,0:T(8,128)(2,1)S(1)}, bf16[32,32,128]{2,1,0:T(8,128)(2,1)S(1)}, u32[]{:S(2)}, u32[]{:S(2)}) collective-permute-start(bf16[32,32,128]{2,1,0:T(8,128)(2,1)S(1)} %collective-permute-done.10), channel_id=1, source_target_pairs={{0,15},{1,0},{2,1},{3,2},{4,3},{5,4},{6,5},{7,6},{8,7},{9,8},{10,9... | collective-permute-start | bytes 786440 | tf_op jit(solution)/shard_map/ppermute | solution.py:21
  56.0 4.1 %collective-permute-done.4 = bf16[32,32,128]{2,1,0:T(8,128)(2,1)S(1)} collective-permute-done((bf16[32,32,128]{2,1,0:T(8,128)(2,1)S(1)}, bf16[32,32,128]{2,1,0:T(8,128)(2,1)S(1)}, u32[]{:S(2)}, u32[]{:S(2)}) %collective-permute-start.4) | collective-permute-done | bytes 262176 | tf_op jit(solution)/shard_map/ppermute | solution.py:19
  60.2 4.5 %collective-permute-start.12 = (bf16[32,32,128]{2,1,0:T(8,128)(2,1)S(1)}, bf16[32,32,128]{2,1,0:T(8,128)(2,1)S(1)}, u32[]{:S(2)}, u32[]{:S(2)}) collective-permute-start(bf16[32,32,128]{2,1,0:T(8,128)(2,1)S(1)} %collective-permute-done.11), channel_id=1, source_target_pairs={{0,15},{1,0},{2,1},{3,2},{4,3},{5,4},{6,5},{7,6},{8,7},{9,8},{10,9... | collective-permute-start | bytes 786440 | tf_op jit(solution)/shard_map/ppermute | solution.py:21
  64.7 4.1 %collective-permute-done.5 = bf16[32,32,128]{2,1,0:T(8,128)(2,1)} collective-permute-done((bf16[32,32,128]{2,1,0:T(8,128)(2,1)S(1)}, bf16[32,32,128]{2,1,0:T(8,128)(2,1)}, u32[]{:S(2)}, u32[]{:S(2)}) %collective-permute-start.5) | collective-permute-done | bytes 262176 | tf_op jit(solution)/shard_map/ppermute | solution.py:19
  69.0 4.5 %collective-permute-start.13 = (bf16[32,32,128]{2,1,0:T(8,128)(2,1)S(1)}, bf16[32,32,128]{2,1,0:T(8,128)(2,1)S(1)}, u32[]{:S(2)}, u32[]{:S(2)}) collective-permute-start(bf16[32,32,128]{2,1,0:T(8,128)(2,1)S(1)} %collective-permute-done.12), channel_id=1, source_target_pairs={{0,15},{1,0},{2,1},{3,2},{4,3},{5,4},{6,5},{7,6},{8,7},{9,8},{10,9... | collective-permute-start | bytes 786440 | tf_op jit(solution)/shard_map/ppermute | solution.py:21
  73.5 4.2 %collective-permute-done.6 = bf16[32,32,128]{2,1,0:T(8,128)(2,1)} collective-permute-done((bf16[32,32,128]{2,1,0:T(8,128)(2,1)}, bf16[32,32,128]{2,1,0:T(8,128)(2,1)}, u32[]{:S(2)}, u32[]{:S(2)}) %collective-permute-start.6) | collective-permute-done | bytes 262176 | tf_op jit(solution)/shard_map/ppermute | solution.py:19
  77.8 1.6 gather_fusion
  79.5 4.7 %collective-permute-start.14 = (bf16[32,32,128]{2,1,0:T(8,128)(2,1)S(1)}, bf16[32,32,128]{2,1,0:T(8,128)(2,1)S(1)}, u32[]{:S(2)}, u32[]{:S(2)}) collective-permute-start(bf16[32,32,128]{2,1,0:T(8,128)(2,1)S(1)} %collective-permute-done.13), channel_id=1, source_target_pairs={{0,15},{1,0},{2,1},{3,2},{4,3},{5,4},{6,5},{7,6},{8,7},{9,8},{10,9... | collective-permute-start | bytes 786440 | tf_op jit(solution)/shard_map/ppermute | solution.py:21
  84.1 2.4 collective-permute-done.7
  87.5 1.0 constant_dynamic-update-slice_fusion.30
  88.5 1.0 constant_dynamic-update-slice_fusion.29
  90.3 1.0 constant_dynamic-update-slice_fusion.15
  94.8 1.9 fusion.4
  97.4 1.0 fusion.12
  98.4 1.0 fusion.13
  99.4 1.0 add_bitcast_fusion
  100.5 3.7 %subtract_bitcast_fusion = f32[6,16,1,128,128]{4,3,1,0,2:T(8,128)} fusion(f32[6,16,128,128]{3,2,1,0:T(8,128)S(1)} %fusion.13, bf16[6,16,2,16,128]{4,1,3,0,2:T(8,128)(2,1)S(1)} %get-tuple-element.10, bf16[6,16,2,16,128]{4,1,3,0,2:T(8,128)(2,1)S(1)} %get-tuple-element.9), kind=kOutput, calls=%fused_computation.6 | convolution fusion | flops 51904512 | bytes 13369344 | tf_op jit(solution)/shard_map/pwfi,pwfj->pfij/dot_general | solution.py:66
  104.2 9.6 %pad_maximum_fusion = f32[6,16,2,128,128]{4,3,1,0,2:T(8,128)} fusion(f32[6,16,1,128,128]{4,3,1,0,2:T(8,128)} %subtract_bitcast_fusion, f32[6,16,1,128,128]{4,3,1,0,2:T(8,128)S(1)} %add_bitcast_fusion), kind=kLoop, calls=%fused_computation.4 | loop fusion | flops 3145728 | bytes 25165824 | tf_op jit(solution)/shard_map/stack | solution.py:72
  113.8 11.3 %copy.19 = f32[6,16,2,128,128]{4,3,0,2,1:T(8,128)} copy(f32[6,16,2,128,128]{4,3,1,0,2:T(8,128)} %pad_maximum_fusion) | data formatting | bytes 25165824
  125.1 14.4 %copy.33 = f32[2,8,1536,128]{3,1,2,0:T(8,128)} copy(f32[2,8,1536,128]{3,2,1,0:T(8,128)} %bitcast.64) | data formatting | bytes 25165824
  139.5 144.3 %reduce-scatter.5.cloned.1.call-done = f32[8,196608]{1,0:T(8,128)} async-done(((f32[16,196608]{1,0:T(8,128)}), f32[8,196608]{1,0:T(8,128)}) %reduce-scatter.5.cloned.1.call-update) | async-done | bytes 6291472
  283.8 4.0 %copy.24 = f32[1,8,1536,128]{3,2,1,0:T(8,128)S(1)} copy(f32[1,8,1536,128]{3,1,2,0:T(8,128)} %bitcast.66) | data formatting | bytes 12582912
  287.8 1.1 copy_multiply_fusion
  289.0 3.1 %copy.18 = f32[6,8,2,128,128]{4,3,2,1,0:T(8,128)} copy(f32[6,8,2,128,128]{4,3,1,0,2:T(8,128)S(1)} %copy_multiply_fusion) | data formatting | bytes 12582912 | tf_op jit(solution)/shard_map/mul | solution.py:95
  (72 shorter events, 7.8 us)
Async XLA Ops:
  6.5 71.3 %copy-start = (s32[1,512]{1,0:T(1,128)S(1)}, s32[1,512]{1,0:T(1,128)}, u32[]{:S(2)}) copy-start(s32[1,512]{1,0:T(1,128)} %param.4) | copy-start | bytes 6148
  6.5 277.3 %reduce-scatter.5.cloned.1.call-start = ((), (), s32[]{:S(2)}) async-start(), calls=%async_computation.1 | async-start | bytes 18874368
  7.2 52.9 %copy-start.2 = (s32[1,6,2]{1,2,0:T(2,128)S(1)}, s32[1,6,2]{1,2,0:T(2,128)}, u32[]{:S(2)}) copy-start(s32[1,6,2]{1,2,0:T(2,128)} %param.5) | copy-start | bytes 148
  16.3 9.5 %collective-permute-start = (bf16[32,32,128]{2,1,0:T(8,128)(2,1)S(1)}, bf16[32,32,128]{2,1,0:T(8,128)(2,1)S(1)}, u32[]{:S(2)}, u32[]{:S(2)}) collective-permute-start(bf16[32,32,128]{2,1,0:T(8,128)(2,1)S(1)} %multiply_convert_fusion), channel_id=1, source_target_pairs={{0,1},{1,2},{2,3},{3,4},{4,5},{5,6},{6,7},{7,8},{8,9},{9,10},{10,1... | collective-permute-start | bytes 786440 | tf_op jit(solution)/shard_map/ppermute | solution.py:19
  25.8 8.5 %collective-permute-start.1 = (bf16[32,32,128]{2,1,0:T(8,128)(2,1)S(1)}, bf16[32,32,128]{2,1,0:T(8,128)(2,1)S(1)}, u32[]{:S(2)}, u32[]{:S(2)}) collective-permute-start(bf16[32,32,128]{2,1,0:T(8,128)(2,1)S(1)} %collective-permute-done), channel_id=1, source_target_pairs={{0,1},{1,2},{2,3},{3,4},{4,5},{5,6},{6,7},{7,8},{8,9},{9,10},{10,1... | collective-permute-start | bytes 786440 | tf_op jit(solution)/shard_map/ppermute | solution.py:19
  25.8 8.5 %collective-permute-start.8 = (bf16[32,32,128]{2,1,0:T(8,128)(2,1)S(1)}, bf16[32,32,128]{2,1,0:T(8,128)(2,1)S(1)}, u32[]{:S(2)}, u32[]{:S(2)}) collective-permute-start(bf16[32,32,128]{2,1,0:T(8,128)(2,1)S(1)} %multiply_convert_fusion), channel_id=1, source_target_pairs={{0,15},{1,0},{2,1},{3,2},{4,3},{5,4},{6,5},{7,6},{8,7},{9,8},{10,9... | collective-permute-start | bytes 786440 | tf_op jit(solution)/shard_map/ppermute | solution.py:21
  34.3 8.6 %collective-permute-start.2 = (bf16[32,32,128]{2,1,0:T(8,128)(2,1)S(1)}, bf16[32,32,128]{2,1,0:T(8,128)(2,1)S(1)}, u32[]{:S(2)}, u32[]{:S(2)}) collective-permute-start(bf16[32,32,128]{2,1,0:T(8,128)(2,1)S(1)} %collective-permute-done.1), channel_id=1, source_target_pairs={{0,1},{1,2},{2,3},{3,4},{4,5},{5,6},{6,7},{7,8},{8,9},{9,10},{10,1... | collective-permute-start | bytes 786440 | tf_op jit(solution)/shard_map/ppermute | solution.py:19
  34.3 8.6 %collective-permute-start.9 = (bf16[32,32,128]{2,1,0:T(8,128)(2,1)S(1)}, bf16[32,32,128]{2,1,0:T(8,128)(2,1)S(1)}, u32[]{:S(2)}, u32[]{:S(2)}) collective-permute-start(bf16[32,32,128]{2,1,0:T(8,128)(2,1)S(1)} %collective-permute-done.8), channel_id=1, source_target_pairs={{0,15},{1,0},{2,1},{3,2},{4,3},{5,4},{6,5},{7,6},{8,7},{9,8},{10,9... | collective-permute-start | bytes 786440 | tf_op jit(solution)/shard_map/ppermute | solution.py:21
  42.9 8.6 %collective-permute-start.3 = (bf16[32,32,128]{2,1,0:T(8,128)(2,1)S(1)}, bf16[32,32,128]{2,1,0:T(8,128)(2,1)S(1)}, u32[]{:S(2)}, u32[]{:S(2)}) collective-permute-start(bf16[32,32,128]{2,1,0:T(8,128)(2,1)S(1)} %collective-permute-done.2), channel_id=1, source_target_pairs={{0,1},{1,2},{2,3},{3,4},{4,5},{5,6},{6,7},{7,8},{8,9},{9,10},{10,1... | collective-permute-start | bytes 786440 | tf_op jit(solution)/shard_map/ppermute | solution.py:19
  42.9 8.6 %collective-permute-start.10 = (bf16[32,32,128]{2,1,0:T(8,128)(2,1)S(1)}, bf16[32,32,128]{2,1,0:T(8,128)(2,1)S(1)}, u32[]{:S(2)}, u32[]{:S(2)}) collective-permute-start(bf16[32,32,128]{2,1,0:T(8,128)(2,1)S(1)} %collective-permute-done.9), channel_id=1, source_target_pairs={{0,15},{1,0},{2,1},{3,2},{4,3},{5,4},{6,5},{7,6},{8,7},{9,8},{10,9... | collective-permute-start | bytes 786440 | tf_op jit(solution)/shard_map/ppermute | solution.py:21
  51.5 8.6 %collective-permute-start.4 = (bf16[32,32,128]{2,1,0:T(8,128)(2,1)S(1)}, bf16[32,32,128]{2,1,0:T(8,128)(2,1)S(1)}, u32[]{:S(2)}, u32[]{:S(2)}) collective-permute-start(bf16[32,32,128]{2,1,0:T(8,128)(2,1)S(1)} %collective-permute-done.3), channel_id=1, source_target_pairs={{0,1},{1,2},{2,3},{3,4},{4,5},{5,6},{6,7},{7,8},{8,9},{9,10},{10,1... | collective-permute-start | bytes 786440 | tf_op jit(solution)/shard_map/ppermute | solution.py:19
  51.5 8.7 %collective-permute-start.11 = (bf16[32,32,128]{2,1,0:T(8,128)(2,1)S(1)}, bf16[32,32,128]{2,1,0:T(8,128)(2,1)S(1)}, u32[]{:S(2)}, u32[]{:S(2)}) collective-permute-start(bf16[32,32,128]{2,1,0:T(8,128)(2,1)S(1)} %collective-permute-done.10), channel_id=1, source_target_pairs={{0,15},{1,0},{2,1},{3,2},{4,3},{5,4},{6,5},{7,6},{8,7},{9,8},{10,9... | collective-permute-start | bytes 786440 | tf_op jit(solution)/shard_map/ppermute | solution.py:21
  60.1 8.7 %collective-permute-start.5 = (bf16[32,32,128]{2,1,0:T(8,128)(2,1)S(1)}, bf16[32,32,128]{2,1,0:T(8,128)(2,1)}, u32[]{:S(2)}, u32[]{:S(2)}) collective-permute-start(bf16[32,32,128]{2,1,0:T(8,128)(2,1)S(1)} %collective-permute-done.4), channel_id=1, source_target_pairs={{0,1},{1,2},{2,3},{3,4},{4,5},{5,6},{6,7},{7,8},{8,9},{9,10},{10,1... | collective-permute-start | bytes 786440 | tf_op jit(solution)/shard_map/ppermute | solution.py:19
  60.2 8.8 %collective-permute-start.12 = (bf16[32,32,128]{2,1,0:T(8,128)(2,1)S(1)}, bf16[32,32,128]{2,1,0:T(8,128)(2,1)S(1)}, u32[]{:S(2)}, u32[]{:S(2)}) collective-permute-start(bf16[32,32,128]{2,1,0:T(8,128)(2,1)S(1)} %collective-permute-done.11), channel_id=1, source_target_pairs={{0,15},{1,0},{2,1},{3,2},{4,3},{5,4},{6,5},{7,6},{8,7},{9,8},{10,9... | collective-permute-start | bytes 786440 | tf_op jit(solution)/shard_map/ppermute | solution.py:21
  68.8 8.9 %collective-permute-start.6 = (bf16[32,32,128]{2,1,0:T(8,128)(2,1)}, bf16[32,32,128]{2,1,0:T(8,128)(2,1)}, u32[]{:S(2)}, u32[]{:S(2)}) collective-permute-start(bf16[32,32,128]{2,1,0:T(8,128)(2,1)} %collective-permute-done.5), channel_id=1, source_target_pairs={{0,1},{1,2},{2,3},{3,4},{4,5},{5,6},{6,7},{7,8},{8,9},{9,10},{10,1... | collective-permute-start | bytes 786440 | tf_op jit(solution)/shard_map/ppermute | solution.py:19
  69.0 10.5 %collective-permute-start.13 = (bf16[32,32,128]{2,1,0:T(8,128)(2,1)S(1)}, bf16[32,32,128]{2,1,0:T(8,128)(2,1)S(1)}, u32[]{:S(2)}, u32[]{:S(2)}) collective-permute-start(bf16[32,32,128]{2,1,0:T(8,128)(2,1)S(1)} %collective-permute-done.12), channel_id=1, source_target_pairs={{0,15},{1,0},{2,1},{3,2},{4,3},{5,4},{6,5},{7,6},{8,7},{9,8},{10,9... | collective-permute-start | bytes 786440 | tf_op jit(solution)/shard_map/ppermute | solution.py:21
  77.7 8.8 %collective-permute-start.7 = (bf16[32,32,128]{2,1,0:T(8,128)(2,1)}, bf16[32,32,128]{2,1,0:T(8,128)(2,1)}, u32[]{:S(2)}, u32[]{:S(2)}) collective-permute-start(bf16[32,32,128]{2,1,0:T(8,128)(2,1)} %collective-permute-done.6), channel_id=1, source_target_pairs={{0,1},{1,2},{2,3},{3,4},{4,5},{5,6},{6,7},{7,8},{8,9},{9,10},{10,1... | collective-permute-start | bytes 786440 | tf_op jit(solution)/shard_map/ppermute | solution.py:19
  79.5 10.7 %collective-permute-start.14 = (bf16[32,32,128]{2,1,0:T(8,128)(2,1)S(1)}, bf16[32,32,128]{2,1,0:T(8,128)(2,1)S(1)}, u32[]{:S(2)}, u32[]{:S(2)}) collective-permute-start(bf16[32,32,128]{2,1,0:T(8,128)(2,1)S(1)} %collective-permute-done.13), channel_id=1, source_target_pairs={{0,15},{1,0},{2,1},{3,2},{4,3},{5,4},{6,5},{7,6},{8,7},{9,8},{10,9... | collective-permute-start | bytes 786440 | tf_op jit(solution)/shard_map/ppermute | solution.py:21
  287.8 4.3 %copy-start.1 = (s32[1,512]{1,0:T(1,128)S(1)}, s32[1,512]{1,0:T(1,128)}, u32[]{:S(2)}) copy-start(s32[1,512]{1,0:T(1,128)} %param.4) | copy-start | bytes 6148
Sparse Core Ops, SparseCore 0:
  139.6 144.1 reduce-scatter.4
